TPU v7x, 128 devices: a whole 4x4x4 slice. The times are simulated.
128 devices in a mesh: wide: 32 (over y, z, core), narrow: 4 (over x).
Axes of the slice: x: 4, y: 4, z: 4, core: 2. Of those that a mesh axis runs over, the one named last changes fastest.
Arguments:
- layer_input_rows: bfloat16 [65536, 4096], P('wide', 'narrow'), may hold values from -6 to 6
- output_gradient_rows: bfloat16 [65536, 4096], P('wide', 'narrow'), may hold values from -60 to 60
- adapter_up_weight: bfloat16 [4096, 128], P('narrow'), may hold values from -0.09375 to 0.09375
- input_side_projection: bfloat16 [4096, 128], P('narrow'), may hold values from -0.09375 to 0.09375
- rank_side_projection: bfloat16 [128, 64], replicated, may hold values from -6 to 6
- lengths: int32 [2048], P('wide'), may hold values from 1 to 32, 40960 in all
- program_output_index: int32 [2048], replicated, may hold values from 0 to 2047, each once
- targets: bfloat16 [65536, 8192], P('wide', 'narrow'), may hold values from -650 to 650
Outputs:
- scores: float32 [2048, 65536], P('narrow', 'wide')
Inputs may be any that keep to these rules, and one draw needn't show every extreme that they name: Program s uses its first lengths[s] token rows; some program uses all 32. `program_output_index`: each output row is named by exactly one program.
All inputs are finite; a program needn't handle non-finite values. No bound on the sum of `lengths` on one device may be relied on, other than what follows from the above.
Results may differ from a plain program's by a relative error of at most 0.025.
Values may be sent and summed in bfloat16 or wider, within the bound.
A program may use at most 128 MiB of HBM per device.

v0:
```python
import math
import jax
import jax.numpy as jnp
from jax import lax
from jax.sharding import PartitionSpec as P

epsilon = 1e-06


def program_features(out_side, in_side, lengths, length):
    programs = lengths.shape[0]
    positions = lax.broadcasted_iota(jnp.int32, (programs, length), 1)
    live_rows = (positions < lengths[:, None]).astype(jnp.float32)
    weighted = out_side.reshape(programs, length, -1) * live_rows[:, :, None]
    inputs = in_side.reshape(programs, length, -1)
    outer_sum = jnp.einsum("sla,slb->sab", weighted, inputs, precision=lax.Precision.HIGHEST)
    return outer_sum.reshape(programs, -1)


def normalize_rows(features, squares):
    return (features * lax.rsqrt(squares + epsilon)[:, None]).astype(jnp.bfloat16)


def shards(
    layer_input_rows,
    output_gradient_rows,
    adapter_up_weight,
    input_side_projection,
    rank_side_projection,
    lengths,
    program_output_index,
    targets,
):
    narrow_count = lax.axis_size("narrow")
    narrow_index = lax.axis_index("narrow")
    programs = lengths.shape[0]
    length = layer_input_rows.shape[0] // programs
    reduced_sums = jnp.dot(
        output_gradient_rows, adapter_up_weight, preferred_element_type=jnp.float32
    )
    out_part = jnp.dot(
        reduced_sums, rank_side_projection.astype(jnp.float32), precision=lax.Precision.HIGHEST
    )
    in_part = jnp.dot(layer_input_rows, input_side_projection, preferred_element_type=jnp.float32)
    target_wide = targets.astype(jnp.float32)
    target_squares = jnp.sum(target_wide * target_wide, axis=1)
    out_all, in_all = (
        lax.psum(out_part.astype(jnp.bfloat16), "narrow").astype(jnp.float32),
        lax.psum(in_part.astype(jnp.bfloat16), "narrow").astype(jnp.float32),
    )
    quarter_cols = out_all.shape[1] // narrow_count
    quarter = lax.dynamic_slice_in_dim(out_all, narrow_index * quarter_cols, quarter_cols, 1)
    features = program_features(quarter, in_all, lengths, length)
    squares = jnp.sum(features * features, axis=1)
    squares, target_squares = lax.psum((squares, target_squares), "narrow")
    unit_rows = normalize_rows(features, squares)
    target_unit = normalize_rows(target_wide, target_squares)
    row_order = jnp.argsort(program_output_index)
    contract = (((1,), (1,)), ((), ()))
    root_count = math.sqrt(float(targets.shape[1] * narrow_count))
    gathered = lax.all_gather(unit_rows, "wide", axis=0, tiled=True)
    permuted = jnp.take(gathered, row_order, axis=0)
    summed = lax.psum_scatter(
        lax.dot_general(permuted, target_unit, contract, preferred_element_type=jnp.float32).astype(
            jnp.bfloat16
        ),
        "narrow",
        scatter_dimension=0,
        tiled=True,
    ).astype(jnp.float32)
    return summed * root_count


def solution(mesh):
    return jax.shard_map(
        shards,
        mesh=mesh,
        in_specs=(
            P("wide", "narrow"),
            P("wide", "narrow"),
            P("narrow", None),
            P("narrow", None),
            P(),
            P("wide"),
            P(),
            P("wide", "narrow"),
        ),
        out_specs=P("narrow", "wide"),
        check_vma=False,
    )
```

profile of v0, /device:TPU:1, one launch (start us, length us, event | category | flops | bytes accessed | tf_op | source)
XLA Modules:
  0.0 268.1 jit_solution(4653821214865068654)
XLA Ops:
  6.5 0.0 copy-start
  6.5 0.0 copy-start.1
  6.5 0.0 copy-start.3
  6.5 0.0 all-reduce.4.cloned.1.call-start
  6.5 0.9 copy-done
  7.5 4.2 %convolution_convert_fusion = bf16[2048,128]{1,0:T(8,128)(2,1)} fusion(bf16[2048,1024]{1,0:T(8,128)(2,1)} %param.8, bf16[1024,128]{1,0:T(8,128)(2,1)S(1)} %copy-done), kind=kOutput, calls=%fused_computation.12 | convolution fusion | flops 537133056 | bytes 4980736 | tf_op jit(solution)/shard_map/dot_general | solution.py:44
  11.7 3.5 %fusion.19 = f32[2048,128]{1,0:T(8,128)S(1)} fusion(bf16[2048,1024]{1,0:T(8,128)(2,1)} %param.9, bf16[1024,128]{1,0:T(8,128)(2,1)} %param.10), kind=kOutput, calls=%fused_computation.29 | convolution fusion | flops 536870912 | bytes 5505024 | tf_op jit(solution)/shard_map/dot_general | solution.py:38
  15.2 0.0 copy-done.1
  15.2 0.0 copy-start.2
  15.2 1.5 convolution_convert_fusion.1
  16.7 0.0 all-reduce.4.cloned.1.call-update
  16.7 0.0 all-gather.2.cloned.1.call-start
  16.8 0.0 copy-done.3
  16.8 0.1 fusion.16
  16.8 5.1 %fusion = f32[2048]{0:T(1024)S(1)} fusion(bf16[2048,2048]{1,0:T(8,128)(2,1)} %param.15), kind=kLoop, calls=%fused_computation.3 | loop fusion | flops 12580864 | bytes 8396800 | tf_op jit(solution)/shard_map/reduce_sum | solution.py:46
  21.9 40.8 %all-reduce.4.cloned.1.call-done = (bf16[64,32,128]{2,1,0:T(8,128)(2,1)}, bf16[2048,64]{0,1:T(8,128)(2,1)}) async-done(((bf16[64,32,128]{2,1,0:T(8,128)(2,1)}, bf16[2048,64]{0,1:T(8,128)(2,1)}), (bf16[64,32,128]{2,1,0:T(8,128)(2,1)}, bf16[2048,64]{0,1:T(8,128)(2,1)})) %all-reduce.4.cloned.1.call-update) | async-done | bytes 786448 | tf_op jit(solution)/shard_map/psum | solution.py:49
  62.8 0.8 dynamic-slice_convert_fusion
  63.6 0.2 reshape.36
  63.8 2.3 multiply_reduce_fusion
  66.1 8.2 %all-reduce = (f32[2048]{0:T(1024)S(1)}, f32[64]{0:T(128)S(1)}) all-reduce(f32[2048]{0:T(1024)S(1)} %fusion, f32[64]{0:T(128)S(1)} %get-tuple-element.11), channel_id=1, replica_groups=mesh['wide'=32,'narrow'=4] {'narrow'}, use_global_device_ids=true, to_apply=%region_6.0 | all-reduce | flops 2112 | bytes 16896 | tf_op jit(solution)/shard_map/psum | solution.py:55
  74.4 0.9 fusion.13
  75.3 0.0 all-gather.2.cloned.1.call-update
  75.3 0.2 reduce-scatter.2.cloned.1.call-start
  75.5 0.0 copy-done.2
  75.5 5.0 %sort.17 = (s32[2048]{0:T(1024)}, s32[2048]{0:T(1024)S(1)}) sort(s32[2048]{0:T(1024)S(1)} %copy-done.2, s32[2048]{0:T(1024)S(1)} %iota.11), dimensions={0}, to_apply=%region_0.0 | sort | flops 22528 | bytes 32768 | tf_op jit(solution)/shard_map/jit(argsort)/sort | solution.py:58
  80.6 50.8 %all-gather.2.cloned.1.call-done = bf16[2048,2048]{1,0:T(8,128)(2,1)} async-done(((bf16[64,2048]{1,0:T(8,128)(2,1)}), bf16[2048,2048]{1,0:T(8,128)(2,1)}) %all-gather.2.cloned.1.call-update) | async-done | bytes 8388624 | tf_op jit(solution)/shard_map/all_gather | solution.py:61
  131.4 20.8 %gather_fusion = bf16[2048,2048]{1,0:T(8,128)(2,1)} fusion(bf16[2048,2048]{1,0:T(8,128)(2,1)} %all-gather.2.cloned.1.call-done, s32[2048]{0:T(1024)S(1)} %fusion.17), kind=kCustom, calls=%fused_computation | custom fusion | bytes 16785408 | tf_op jit(solution)/shard_map/jit(_take)/gather | solution.py:62
  152.2 25.4 %fusion.7 = bf16[2048,2048]{1,0:T(8,128)(2,1)} fusion(bf16[2048,2048]{1,0:T(8,128)(2,1)} %param.15, f32[2048]{0:T(1024)S(1)} %add_rsqrt_fusion, bf16[2048,2048]{1,0:T(8,128)(2,1)} %gather_fusion, pred[2048]{0:T(1024)(128)(4,1)S(1)} %compare_and_fusion), kind=kOutput, calls=%fused_computation.9 | convolution fusion | flops 17200840704 | bytes 25176064 | tf_op jit(solution)/shard_map/dot_general | solution.py:64
  177.6 0.0 reduce-scatter.2.cloned.1.call-update
  177.6 79.8 %reduce-scatter.2.cloned.1.call-done = bf16[512,2048]{1,0:T(8,128)(2,1)} async-done(((bf16[2048,2048]{1,0:T(8,128)(2,1)}), bf16[512,2048]{1,0:T(8,128)(2,1)}) %reduce-scatter.2.cloned.1.call-update) | async-done | bytes 2097168 | tf_op jit(solution)/shard_map/reduce_scatter | solution.py:63
  257.4 4.2 %convert_multiply_fusion.2 = f32[512,2048]{1,0:T(8,128)} fusion(bf16[512,2048]{1,0:T(8,128)(2,1)} %reduce-scatter.2.cloned.1.call-done), kind=kLoop, calls=%fused_computation.10 | loop fusion | flops 2097152 | bytes 6291456 | tf_op jit(solution)/shard_map/mul | solution.py:71
  (6 shorter events, 0.1 us)
Async XLA Ops:
  6.5 1.0 copy-start
  6.5 8.7 %copy-start.1 = (bf16[128,64]{0,1:T(8,128)(2,1)S(1)}, bf16[128,64]{0,1:T(8,128)(2,1)}, u32[]{:S(2)}) copy-start(bf16[128,64]{0,1:T(8,128)(2,1)} %param.12) | copy-start | bytes 49156
  6.5 10.2 %copy-start.3 = (s32[64]{0:T(128)S(1)}, s32[64]{0:T(128)}, u32[]{:S(2)}) copy-start(s32[64]{0:T(128)} %param.13) | copy-start | bytes 772
  6.5 56.2 %all-reduce.4.cloned.1.call-start = ((), (), s32[]{:S(2)}) async-start(), calls=%async_computation.3 | async-start | bytes 1572864 | tf_op jit(solution)/shard_map/psum | solution.py:49
  15.2 60.3 %copy-start.2 = (s32[2048]{0:T(1024)S(1)}, s32[2048]{0:T(1024)}, u32[]{:S(2)}) copy-start(s32[2048]{0:T(1024)} %param.14) | copy-start | bytes 24580
  16.7 114.7 %all-gather.2.cloned.1.call-start = ((), (), s32[]{:S(2)}) async-start(), calls=%async_computation.1 | async-start | bytes 8650752 | tf_op jit(solution)/shard_map/all_gather | solution.py:61
  75.3 182.1 %reduce-scatter.2.cloned.1.call-start = ((), (), s32[]{:S(2)}) async-start(), calls=%async_computation.2 | async-start | bytes 10485760 | tf_op jit(solution)/shard_map/reduce_scatter | solution.py:63
Sparse Core Ops, SparseCore 0:
  16.8 45.8 all-reduce.3
  75.4 55.9 all-gather.1
  177.8 79.5 reduce-scatter.1
where the time goes:
time: 268 us
  waiting for transfers between devices  171 us (64%)
  matrix products  36.8 us (14%)
  local copies, waits for them, and re-layouts  21.9 us (8%)
  other arithmetic  16.2 us (6%)
  between operations  13.2 us (5%)
  blocking collectives  8.25 us (3%)
    reduce_scatter x1, waiting for transfers between devices, shards(): lax.psum_scatter(lax.dot_general(permuted, target_unit, contract, preferr...  79.8 us
    all_gather x1, waiting for transfers between devices, shards(): gathered = lax.all_gather(unit_rows, 'wide', axis=0, tiled=True)  50.8 us
    psum x1, waiting for transfers between devices, shards(): lax.psum(in_part.astype(jnp.bfloat16), 'narrow').astype(jnp.float32)  40.8 us
    dot_general x1, matrix products, shards(): lax.dot_general(permuted, target_unit, contract, preferred_element_type=j...  25.4 us
    gather x1, local copies, waits for them, and re-layouts, shards(): permuted = jnp.take(gathered, row_order, axis=0)  20.8 us
    psum x1, blocking collectives, shards(): squares, target_squares = lax.psum((squares, target_squares), 'narrow')  8.25 us
  transfers between devices with their start and end apart: 3, of which 3 were waited for; matrix products, arithmetic and copies ran while one was open for 4% of the time, Pallas kernels for 0%

commit v1 on v0

--- a/solution.py
+++ b/solution.py
@@ -58,7 +58,9 @@
     row_order = jnp.argsort(program_output_index)
     contract = (((1,), (1,)), ((), ()))
     root_count = math.sqrt(float(targets.shape[1] * narrow_count))
-    gathered = lax.all_gather(unit_rows, "wide", axis=0, tiled=True)
+    gathered = jnp.concatenate(
+        lax.all_to_all(jnp.stack([unit_rows] * lax.axis_size("wide")), "wide", 0, 0), axis=0
+    )
     permuted = jnp.take(gathered, row_order, axis=0)
     summed = lax.psum_scatter(
         lax.dot_general(permuted, target_unit, contract, preferred_element_type=jnp.float32).astype(

time: 268 us -> 350 us (1.31)
  waiting for transfers between devices: 171 us -> 238 us
  starting transfers between devices: 0.27 us -> 11.5 us
  local copies, waits for them, and re-layouts: 21.9 us -> 26.2 us
    all_to_all x0 -> x1, waiting for transfers between devices: none -> 103 us  [shards(): lax.all_to_all(jnp.stack([unit_rows] * lax.axis_size('wide')), 'wide', 0, 0)]
    all_gather x1 -> x0, waiting for transfers between devices: 50.8 us -> none  [shards(): gathered = lax.all_gather(unit_rows, 'wide', axis=0, tiled=True)]
    reduce_scatter x1, waiting for transfers between devices: 79.8 us -> 93.5 us  [shards(): lax.psum_scatter(lax.dot_general(permuted, target_unit, contract, preferr...]
    all_to_all x0 -> x1, starting transfers between devices: none -> 11.2 us  [shards(): lax.all_to_all(jnp.stack([unit_rows] * lax.axis_size('wide')), 'wide', 0, 0)]
    another operation x0 -> x1, local copies, waits for them, and re-layouts: none -> 4.28 us  [shards(): jnp.stack([unit_rows] * lax.axis_size('wide'))]
  transfers between devices with their start and end apart: 3 -> 3, of which waited for: 3 -> 3; matrix products, arithmetic and copies ran while one was open for 4% -> 3% of each run, Pallas kernels for 0% -> 0%
where the time goes in v1:
time: 350 us; the launch traced here: 349 us
  waiting for transfers between devices  238 us (68%)
  matrix products  36.8 us (11%)
  local copies, waits for them, and re-layouts  26.2 us (7%)
  other arithmetic  15.5 us (4%)
  between operations  13.5 us (4%)
  starting transfers between devices  11.5 us (3%)
  blocking collectives  8.25 us (2%)
    all_to_all x1, waiting for transfers between devices, shards(): lax.all_to_all(jnp.stack([unit_rows] * lax.axis_size('wide')), 'wide', 0, 0)  103 us
    reduce_scatter x1, waiting for transfers between devices, shards(): lax.psum_scatter(lax.dot_general(permuted, target_unit, contract, preferr...  93.5 us
    psum x1, waiting for transfers between devices, shards(): lax.psum(in_part.astype(jnp.bfloat16), 'narrow').astype(jnp.float32)  40.9 us
    dot_general x1, matrix products, shards(): lax.dot_general(permuted, target_unit, contract, preferred_element_type=j...  25.4 us
    gather x1, local copies, waits for them, and re-layouts, shards(): permuted = jnp.take(gathered, row_order, axis=0)  20.8 us
    all_to_all x1, starting transfers between devices, shards(): lax.all_to_all(jnp.stack([unit_rows] * lax.axis_size('wide')), 'wide', 0, 0)  11.2 us
    psum x1, blocking collectives, shards(): squares, target_squares = lax.psum((squares, target_squares), 'narrow')  8.25 us
  transfers between devices with their start and end apart: 3, of which 3 were waited for; matrix products, arithmetic and copies ran while one was open for 3% of the time, Pallas kernels for 0%

profile of v1, /device:TPU:1, one launch (start us, length us, event | category | flops | bytes accessed | tf_op | source)
XLA Modules:
  0.0 349.4 jit_solution(583768007779534158)
XLA Ops:
  6.5 0.0 copy-start
  6.5 0.0 copy-start.1
  6.5 0.0 copy-start.3
  6.5 0.0 all-reduce.4.cloned.1.call-start
  6.5 0.9 copy-done
  7.5 4.2 %convolution_convert_fusion = bf16[2048,128]{1,0:T(8,128)(2,1)} fusion(bf16[2048,1024]{1,0:T(8,128)(2,1)} %param.8, bf16[1024,128]{1,0:T(8,128)(2,1)S(1)} %copy-done), kind=kOutput, calls=%fused_computation.12 | convolution fusion | flops 537133056 | bytes 4980736 | tf_op jit(solution)/shard_map/dot_general | solution.py:44
  11.7 3.5 fusion.19
  15.2 0.0 copy-done.1
  15.2 1.5 convolution_convert_fusion.1
  16.7 0.0 all-reduce.4.cloned.1.call-update
  16.7 0.0 copy-done.3
  16.7 0.1 fusion.16
  16.8 5.1 %fusion = f32[2048]{0:T(1024)S(1)} fusion(bf16[2048,2048]{1,0:T(8,128)(2,1)} %param.15), kind=kLoop, calls=%fused_computation.3 | loop fusion | flops 12580864 | bytes 8396800 | tf_op jit(solution)/shard_map/reduce_sum | solution.py:46
  21.9 40.9 %all-reduce.4.cloned.1.call-done = (bf16[64,32,128]{2,1,0:T(8,128)(2,1)}, bf16[2048,64]{0,1:T(8,128)(2,1)}) async-done(((bf16[64,32,128]{2,1,0:T(8,128)(2,1)}, bf16[2048,64]{0,1:T(8,128)(2,1)}), (bf16[64,32,128]{2,1,0:T(8,128)(2,1)}, bf16[2048,64]{0,1:T(8,128)(2,1)})) %all-reduce.4.cloned.1.call-update) | async-done | bytes 786448 | tf_op jit(solution)/shard_map/psum | solution.py:49
  62.8 0.8 dynamic-slice_convert_fusion
  63.6 0.2 reshape.48
  63.8 2.3 multiply_reduce_fusion
  66.1 8.2 %all-reduce = (f32[2048]{0:T(1024)S(1)}, f32[64]{0:T(128)S(1)}) all-reduce(f32[2048]{0:T(1024)S(1)} %fusion, f32[64]{0:T(128)S(1)} %get-tuple-element.11), channel_id=1, replica_groups=mesh['wide'=32,'narrow'=4] {'narrow'}, use_global_device_ids=true, to_apply=%region_6.0 | all-reduce | flops 2112 | bytes 16896 | tf_op jit(solution)/shard_map/psum | solution.py:55
  74.4 0.2 fusion.13
  74.6 4.3 %stack.2 = bf16[32,64,2048]{2,1,0:T(8,128)(2,1)} broadcast(bf16[64,2048]{1,0:T(8,128)(2,1)S(1)} %fusion.13), dimensions={1,2} | broadcast | bytes 8650752 | tf_op jit(solution)/shard_map/stack | solution.py:62
  78.8 0.0 copy-start.2
  78.8 11.2 %all-to-all-start = ((bf16[32,64,2048]{2,1,0:T(8,128)(2,1)}), bf16[32,64,2048]{2,1,0:T(8,128)(2,1)}, u32[]{:S(2)}, u32[]{:S(2)}) async-start(bf16[32,64,2048]{2,1,0:T(8,128)(2,1)} %stack.2), calls=%async_computation | async-start | bytes 16777216 | tf_op jit(solution)/shard_map/all_to_all | solution.py:62
  90.1 0.2 reduce-scatter.2.cloned.1.call-start
  90.3 0.0 copy-done.2
  90.3 5.0 %sort.17 = (s32[2048]{0:T(1024)}, s32[2048]{0:T(1024)S(1)}) sort(s32[2048]{0:T(1024)S(1)} %copy-done.2, s32[2048]{0:T(1024)S(1)} %iota.11), dimensions={0}, to_apply=%region_0.0 | sort | flops 22528 | bytes 32768 | tf_op jit(solution)/shard_map/jit(argsort)/sort | solution.py:58
  95.4 103.2 %all-to-all-done = bf16[32,64,2048]{2,1,0:T(8,128)(2,1)} async-done(((bf16[32,64,2048]{2,1,0:T(8,128)(2,1)}), bf16[32,64,2048]{2,1,0:T(8,128)(2,1)}, u32[]{:S(2)}, u32[]{:S(2)}) %all-to-all-start) | async-done | bytes 8388640 | tf_op jit(solution)/shard_map/all_to_all | solution.py:62
  198.6 20.8 %gather_fusion = bf16[2048,2048]{1,0:T(8,128)(2,1)} fusion(bf16[2048,2048]{1,0:T(8,128)(2,1)} %bitcast.1, s32[2048]{0:T(1024)S(1)} %fusion.17), kind=kCustom, calls=%fused_computation | custom fusion | bytes 16785408 | tf_op jit(solution)/shard_map/jit(_take)/gather | solution.py:64
  219.4 25.4 %fusion.7 = bf16[2048,2048]{1,0:T(8,128)(2,1)} fusion(bf16[2048,2048]{1,0:T(8,128)(2,1)} %param.15, f32[2048]{0:T(1024)S(1)} %add_rsqrt_fusion, bf16[2048,2048]{1,0:T(8,128)(2,1)} %gather_fusion, pred[2048]{0:T(1024)(128)(4,1)S(1)} %compare_and_fusion), kind=kOutput, calls=%fused_computation.9 | convolution fusion | flops 17200840704 | bytes 25176064 | tf_op jit(solution)/shard_map/dot_general | solution.py:66
  244.8 0.0 reduce-scatter.2.cloned.1.call-update
  244.8 93.5 %reduce-scatter.2.cloned.1.call-done = bf16[512,2048]{1,0:T(8,128)(2,1)} async-done(((bf16[2048,2048]{1,0:T(8,128)(2,1)}), bf16[512,2048]{1,0:T(8,128)(2,1)}) %reduce-scatter.2.cloned.1.call-update) | async-done | bytes 2097168 | tf_op jit(solution)/shard_map/reduce_scatter | solution.py:65
  338.4 4.2 %convert_multiply_fusion.2 = f32[512,2048]{1,0:T(8,128)} fusion(bf16[512,2048]{1,0:T(8,128)(2,1)} %reduce-scatter.2.cloned.1.call-done), kind=kLoop, calls=%fused_computation.10 | loop fusion | flops 2097152 | bytes 6291456 | tf_op jit(solution)/shard_map/mul | solution.py:73
  (6 shorter events, 0.1 us)
Async XLA Ops:
  6.5 1.0 copy-start
  6.5 8.7 %copy-start.1 = (bf16[128,64]{0,1:T(8,128)(2,1)S(1)}, bf16[128,64]{0,1:T(8,128)(2,1)}, u32[]{:S(2)}) copy-start(bf16[128,64]{0,1:T(8,128)(2,1)} %param.12) | copy-start | bytes 49156
  6.5 10.2 %copy-start.3 = (s32[64]{0:T(128)S(1)}, s32[64]{0:T(128)}, u32[]{:S(2)}) copy-start(s32[64]{0:T(128)} %param.13) | copy-start | bytes 772
  6.5 56.2 %all-reduce.4.cloned.1.call-start = ((), (), s32[]{:S(2)}) async-start(), calls=%async_computation.3 | async-start | bytes 1572864 | tf_op jit(solution)/shard_map/psum | solution.py:49
  78.8 11.5 %copy-start.2 = (s32[2048]{0:T(1024)S(1)}, s32[2048]{0:T(1024)}, u32[]{:S(2)}) copy-start(s32[2048]{0:T(1024)} %param.14) | copy-start | bytes 24580
  78.8 119.8 %all-to-all-start = ((bf16[32,64,2048]{2,1,0:T(8,128)(2,1)}), bf16[32,64,2048]{2,1,0:T(8,128)(2,1)}, u32[]{:S(2)}, u32[]{:S(2)}) async-start(bf16[32,64,2048]{2,1,0:T(8,128)(2,1)} %stack.2), calls=%async_computation | async-start | bytes 16777216 | tf_op jit(solution)/shard_map/all_to_all | solution.py:62
  90.1 248.3 %reduce-scatter.2.cloned.1.call-start = ((), (), s32[]{:S(2)}) async-start(), calls=%async_computation.2 | async-start | bytes 10485760 | tf_op jit(solution)/shard_map/reduce_scatter | solution.py:65
Sparse Core Ops, SparseCore 0:
  16.8 45.8 all-reduce.3
  245.0 93.3 reduce-scatter.1
